TPU v7x, 32 devices: a whole 2x2x4 slice. The times are simulated.
32 devices in a mesh: dp: 16 (over z, y, core), seq: 2 (over x).
Axes of the slice: x: 2, y: 2, z: 4, core: 2. Of those that a mesh axis runs over, the one named last changes fastest.
Arguments:
- queries: bfloat16 [4096, 1536], P(('dp', 'seq')), may hold values from -5 to 5
- keys: bfloat16 [4096, 1536], P(('dp', 'seq')), may hold values from -5 to 5
- values: bfloat16 [4096, 1536], P(('dp', 'seq')), may hold values from -6 to 6
- upstream: bfloat16 [4096, 1536], P(('dp', 'seq')), may hold values from -6 to 6
- out_weight: bfloat16 [1536, 1536], P('dp'), may hold values from -0.15625 to 0.15625
- clip_shape: int32 [16, 2, 3], P('dp'), may hold values from 1 to 3, as said below
- slot_tile: int32 [16, 8], P('dp'), may hold values from 0 to 7, each once within a row
Outputs:
- mixed_out: bfloat16 [4096, 1536], P(('dp', 'seq'))
- query_grad: bfloat16 [4096, 1536], P(('dp', 'seq'))
- key_grad: bfloat16 [4096, 1536], P(('dp', 'seq'))
- value_grad: bfloat16 [4096, 1536], P(('dp', 'seq'))
- weight_grad: float32 [1536, 1536], P('dp')
Inputs may be any that keep to these rules, and one draw needn't show every extreme that they name: `clip_shape`: in every batch the clips' tile counts add up to 8; a clip is 1 or 2 tiles long in time and 2 tiles high.
All inputs are finite; a program needn't handle non-finite values.
Results may differ from a plain program's by a relative error of at most 0.02.
Values may be sent and summed in bfloat16 or wider, within the bound.
No kernel may reach another device: no remote copies, remote signals or barrier semaphores. Data moves between devices by JAX's collectives and lax.ppermute only.
A program may use at most 128 MiB of HBM per device.

v0:
```python
import jax
import jax.numpy as jnp
from jax import lax
from jax.sharding import PartitionSpec as P

HEADS = 12
HEAD_DIM = 128
TILE = 32


def tile_place(clip_dims, tile_ids):
    clip_sizes = clip_dims[:, 0] * clip_dims[:, 1] * clip_dims[:, 2]
    clip_starts = jnp.cumsum(clip_sizes) - clip_sizes
    clip_of = jnp.sum((tile_ids[:, None] >= clip_starts[None, :]).astype(jnp.int32), axis=1) - 1
    chooser = (clip_of[:, None] == jnp.arange(clip_dims.shape[0], dtype=jnp.int32)[None, :]).astype(
        jnp.int32
    )
    first_tile = jnp.sum(chooser * clip_starts[None, :], axis=1)
    high_tiles = jnp.sum(chooser * clip_dims[None, :, 1], axis=1)
    wide_tiles = jnp.sum(chooser * clip_dims[None, :, 2], axis=1)
    offset = tile_ids - first_tile
    return (
        clip_of,
        offset // (wide_tiles * high_tiles),
        offset // wide_tiles % high_tiles,
        offset % wide_tiles,
    )


def tile_window(place_rows, place_cols):
    inside = place_rows[0][:, None] == place_cols[0][None, :]
    for dimension in range(1, 4):
        inside = inside & (
            jnp.abs(place_rows[dimension][:, None] - place_cols[dimension][None, :]) <= 1
        )
    return inside


def per_device(queries, keys, values, upstream, out_weight, clip_shape, slot_tile):
    row_count = queries.shape[0]
    feat_count = queries.shape[1]
    scaling = HEAD_DIM ** (-0.5)
    clip_dims = clip_shape[0]
    slot_list = slot_tile[0]
    local_tiles = row_count // TILE
    own_seat = lax.axis_index("seq")
    own_slots = lax.dynamic_slice_in_dim(slot_list, own_seat * local_tiles, local_tiles)
    own_tokens = own_slots[jnp.arange(row_count, dtype=jnp.int32) // TILE]
    all_tokens = slot_list[jnp.arange(slot_list.shape[0] * TILE, dtype=jnp.int32) // TILE]
    own_place = tile_place(clip_dims, own_tokens)
    all_place = tile_place(clip_dims, all_tokens)
    allowed = tile_window(own_place, all_place)
    full_weight = lax.all_gather(out_weight, "dp", axis=0, tiled=True)
    key_all, value_all = (
        lax.all_gather(keys, "seq", axis=0, tiled=True),
        lax.all_gather(values, "seq", axis=0, tiled=True),
    )
    group_tokens = key_all.shape[0]
    query3 = queries.reshape(row_count, HEADS, HEAD_DIM)
    key_all3 = key_all.reshape(group_tokens, HEADS, HEAD_DIM)
    value_all3 = value_all.reshape(group_tokens, HEADS, HEAD_DIM)
    scores = (
        jnp.einsum("ihd,jhd->hij", query3, key_all3, preferred_element_type=jnp.float32) * scaling
    )
    scores = jnp.where(allowed[None], scores, -jnp.inf)
    row_max = jnp.max(scores, axis=2)
    exponent = jnp.exp(scores - row_max[:, :, None])
    row_sum = jnp.sum(exponent, axis=2)
    weights = exponent.astype(jnp.bfloat16)
    mixed = (
        jnp.einsum("hij,jhd->ihd", weights, value_all3, preferred_element_type=jnp.float32)
        / jnp.transpose(row_sum)[:, :, None]
    )
    attended = mixed.reshape(row_count, feat_count).astype(jnp.bfloat16)
    mixed_out = jnp.einsum(
        "id,od->io", attended, full_weight, preferred_element_type=jnp.float32
    ).astype(jnp.bfloat16)
    grad_out = jnp.dot(upstream, full_weight, preferred_element_type=jnp.float32).astype(
        jnp.bfloat16
    )
    grad3 = grad_out.reshape(row_count, HEADS, HEAD_DIM)
    attended3 = attended.reshape(row_count, HEADS, HEAD_DIM)
    inner_sum = jnp.transpose(
        jnp.sum(grad3.astype(jnp.float32) * attended3.astype(jnp.float32), axis=2)
    )
    log_total = row_max + jnp.log(row_sum)
    prob_full = jnp.exp(scores - log_total[:, :, None])
    slope = jnp.einsum("ihd,jhd->hij", grad3, value_all3, preferred_element_type=jnp.float32)
    score_grad = (prob_full * (slope - inner_sum[:, :, None])).astype(jnp.bfloat16)
    query_grad = (
        (
            jnp.einsum("hij,jhd->ihd", score_grad, key_all3, preferred_element_type=jnp.float32)
            * scaling
        )
        .reshape(row_count, feat_count)
        .astype(jnp.bfloat16)
    )
    prob_low = prob_full.astype(jnp.bfloat16)
    key_part = (
        jnp.einsum("hij,ihd->jhd", score_grad, query3, preferred_element_type=jnp.float32) * scaling
    )
    value_part = jnp.einsum("hij,ihd->jhd", prob_low, grad3, preferred_element_type=jnp.float32)
    key_value_grad = lax.psum_scatter(
        jnp.concatenate(
            [
                key_part.reshape(row_count * lax.axis_size("seq"), feat_count),
                value_part.reshape(row_count * lax.axis_size("seq"), feat_count),
            ],
            axis=1,
        ),
        "seq",
        scatter_dimension=0,
        tiled=True,
    )
    key_grad = key_value_grad[:, :feat_count].astype(jnp.bfloat16)
    value_grad = key_value_grad[:, feat_count:].astype(jnp.bfloat16)
    grad_piece = lax.psum_scatter(
        jnp.einsum("io,id->od", upstream, attended, preferred_element_type=jnp.float32),
        "dp",
        scatter_dimension=0,
        tiled=True,
    )
    weight_grad = lax.psum(grad_piece, "seq")
    return (mixed_out, query_grad, key_grad, value_grad, weight_grad)


def solution(mesh):
    return jax.shard_map(
        per_device,
        mesh=mesh,
        in_specs=(
            P(("dp", "seq"), None),
            P(("dp", "seq"), None),
            P(("dp", "seq"), None),
            P(("dp", "seq"), None),
            P("dp", None),
            P("dp", None, None),
            P("dp", None),
        ),
        out_specs=(
            P(("dp", "seq"), None),
            P(("dp", "seq"), None),
            P(("dp", "seq"), None),
            P(("dp", "seq"), None),
            P("dp", None),
        ),
        check_vma=False,
    )
```

profile of v0, /device:TPU:0, one launch (start us, length us, event | category | flops | bytes accessed | tf_op | source)
XLA Modules:
  0.0 287.7 jit_solution(4399860673712116079)
XLA Ops:
  7.2 0.7 all-gather.2.cloned.1.call-update
  8.0 1.0 slice_reduce_fusion.1
  9.0 0.1 reduce
  9.1 1.2 copy.47
  10.4 1.4 copy.48
  11.8 12.8 %all_gather.10 = bf16[256,1536]{1,0:T(8,128)(2,1)S(1)} all-gather(bf16[128,1536]{1,0:T(8,128)(2,1)S(1)} %copy-done.7), channel_id=1, replica_groups=mesh['dp'=16,'seq'=2] {'seq'}, dimensions={0}, use_global_device_ids=true | all-gather | bytes 1179648 | tf_op jit(solution)/shard_map/all_gather | solution.py:56
  24.5 1.2 copy.51
  25.7 0.1 constant_dynamic-slice_fusion
  25.8 0.7 fusion.18
  26.5 2.5 fusion.16
  29.0 0.6 fusion.19
  29.6 4.4 %compare_select_fusion.1 = s32[256,1]{0,1:T(1,128)S(1)} fusion(s32[]{:T(128)} %bitcast.7, s32[]{:T(128)} %bitcast.8, s32[]{:T(128)} %bitcast.9, s32[]{:T(128)} %bitcast.10, s32[]{:T(128)} %bitcast.11, s32[]{:T(128)} %bitcast.13, s32[]{:T(128)} %bitcast.12), kind=kLoop, calls=%fused_computation.30 | loop fusion | flops 5888 | bytes 1052 | tf_op jit(solution)/shard_map/gather | solution.py:49
  34.1 0.1 fusion.15
  34.2 0.6 broadcast_select_fusion
  34.8 0.1 fusion.14
  34.9 0.1 select_reduce_fusion.3
  35.0 0.1 select_reduce_fusion
  35.1 11.0 %all_gather.9 = bf16[256,1536]{0,1:T(8,128)(2,1)S(1)} all-gather(bf16[128,1536]{0,1:T(8,128)(2,1)S(1)} %copy.48), channel_id=1, replica_groups=mesh['dp'=16,'seq'=2] {'seq'}, dimensions={0}, use_global_device_ids=true | all-gather | bytes 1179648 | tf_op jit(solution)/shard_map/all_gather | solution.py:55
  46.1 2.8 and_select_fusion.8
  48.8 0.3 and_select_fusion.7
  49.1 0.2 fusion.13
  49.3 0.5 fusion.20
  49.8 0.5 fusion
  50.3 15.7 %all-gather.2.cloned.1.call-done = bf16[1536,1536]{1,0:T(8,128)(2,1)} async-done(((bf16[96,1536]{1,0:T(8,128)(2,1)}), bf16[1536,1536]{1,0:T(8,128)(2,1)}) %all-gather.2.cloned.1.call-update) | async-done | bytes 4718608 | tf_op jit(solution)/shard_map/all_gather | solution.py:53
  66.0 3.1 %convolution_convert_fusion = bf16[128,1536]{1,0:T(8,128)(2,1)S(1)} fusion(bf16[128,1536]{1,0:T(8,128)(2,1)S(1)} %copy-done, bf16[1536,1536]{1,0:T(8,128)(2,1)} %all-gather.2.cloned.1.call-done), kind=kOutput, calls=%fused_computation.2 | convolution fusion | flops 604176384 | bytes 5505024 | tf_op jit(solution)/shard_map/dot_general | solution.py:78
  69.1 0.2 copy.52
  69.3 2.4 multiply_reduce_fusion
  71.7 0.7 copy-done.5
  72.5 5.0 %convolution_bitcast_fusion = f32[1536,1536]{0,1:T(8,128)} fusion(bf16[128,1536]{0,1:T(8,128)(2,1)S(1)} %bitcast.70, bf16[128,1536]{1,0:T(8,128)(2,1)S(1)} %copy-done), kind=kOutput, calls=%fused_computation | convolution fusion | flops 603979776 | bytes 10223616 | tf_op jit(solution)/shard_map/io,id->od/dot_general | solution.py:118
  77.5 9.6 %copy.63 = f32[1536,1536]{1,0:T(8,128)} copy(f32[1536,1536]{0,1:T(8,128)} %convolution_bitcast_fusion) | data formatting | bytes 18874368
  87.2 0.6 copy-done.9
  87.9 1.6 fusion.6
  89.5 3.1 %copy.56 = f32[256,1536]{1,0:T(8,128)} copy(f32[256,1536]{0,1:T(8,128)} %bitcast.61) | data formatting | bytes 3145728 | tf_op jit(solution)/shard_map/reshape | solution.py:107
  92.5 2.1 multiply_convert_fusion
  94.7 1.5 convolution_multiply_fusion
  96.2 3.4 %copy.55 = f32[256,1536]{1,0:T(8,128)} copy(f32[256,1536]{0,1:T(8,128)} %bitcast.62) | data formatting | bytes 3145728 | tf_op jit(solution)/shard_map/reshape | solution.py:106
  99.5 3.5 %pad_maximum_fusion = f32[256,3072]{1,0:T(8,128)} fusion(f32[256,1536]{1,0:T(8,128)S(1)} %copy-done.1, f32[256,1536]{1,0:T(8,128)} %copy.55), kind=kLoop, calls=%fused_computation.1 | loop fusion | flops 786432 | bytes 6291456 | tf_op jit(solution)/shard_map/concatenate | solution.py:104
  103.1 1.0 copy-done.6
  104.0 5.3 %convolution_convert_fusion.1 = bf16[128,1536]{1,0:T(8,128)(2,1)} fusion(bf16[128,1536]{0,1:T(8,128)(2,1)S(1)} %bitcast.71, bf16[1536,1536]{1,0:T(8,128)(2,1)} %all-gather.2.cloned.1.call-done), kind=kOutput, calls=%fused_computation.3 | convolution fusion | flops 604176384 | bytes 5505024 | tf_op jit(solution)/shard_map/id,od->io/dot_general | solution.py:75
  109.3 87.8 %reduce-scatter.7.cloned.1.call-done = f32[96,1536]{1,0:T(8,128)} async-done(((f32[1536,1536]{1,0:T(8,128)}), f32[96,1536]{1,0:T(8,128)}) %reduce-scatter.7.cloned.1.call-update) | async-done | bytes 589840
  197.1 2.2 copy.64
  199.3 0.4 fusion.4
  199.7 0.9 copy.57
  200.6 41.8 %reduce-scatter.5.cloned.1.call-done = f32[128,3072]{1,0:T(8,128)} async-done(((f32[256,3072]{1,0:T(8,128)}), f32[128,3072]{1,0:T(8,128)}) %reduce-scatter.5.cloned.1.call-update) | async-done | bytes 1572880 | tf_op jit(solution)/shard_map/reduce_scatter | solution.py:103
  242.4 1.5 convert.4
  243.9 0.9 fusion.17
  244.9 34.1 %all-reduce.2.cloned.1.call-done = f32[96,1536]{0,1:T(8,128)} async-done(((f32[96,1536]{0,1:T(8,128)}), f32[96,1536]{0,1:T(8,128)}) %all-reduce.2.cloned.1.call-update) | async-done | bytes 589840 | tf_op jit(solution)/shard_map/psum | solution.py:123
  279.0 2.2 copy.58
  (34 shorter events, 0.4 us)
Async XLA Ops:
  7.2 58.8 %copy-start = (bf16[128,1536]{1,0:T(8,128)(2,1)S(1)}, bf16[128,1536]{1,0:T(8,128)(2,1)}, u32[]{:S(2)}) copy-start(bf16[128,1536]{1,0:T(8,128)(2,1)} %param.10) | copy-start | bytes 1179652
  7.2 4.6 %copy-start.7 = (bf16[128,1536]{1,0:T(8,128)(2,1)S(1)}, bf16[128,1536]{1,0:T(8,128)(2,1)}, u32[]{:S(2)}) copy-start(bf16[128,1536]{1,0:T(8,128)(2,1)} %param.9) | copy-start | bytes 1179652
  7.2 58.8 %all-gather.2.cloned.1.call-start = ((), (), s32[]{:S(2)}) async-start(), calls=%async_computation.2 | async-start | bytes 5013504 | tf_op jit(solution)/shard_map/all_gather | solution.py:53
  7.9 189.2 %reduce-scatter.7.cloned.1.call-start = ((), (), s32[]{:S(2)}) async-start(), calls=%async_computation.5 | async-start | bytes 10027008
  10.4 38.9 %copy-start.3 = (bf16[128,1536]{0,1:T(8,128)(2,1)}, bf16[128,1536]{0,1:T(8,128)(2,1)S(1)}, u32[]{:S(2)}) copy-start(bf16[128,1536]{0,1:T(8,128)(2,1)S(1)} %copy.47) | copy-start | bytes 1179652
  11.8 14.0 %copy-start.10 = (s32[1,8]{1,0:T(1,128)S(1)}, s32[1,8]{1,0:T(1,128)}, u32[]{:S(2)}) copy-start(s32[1,8]{1,0:T(1,128)} %param.13) | copy-start | bytes 100
  50.3 19.0 %copy-start.8 = (f32[12,128]{1,0:T(8,128)}, f32[12,128]{1,0:T(8,128)S(1)}, u32[]{:S(2)}) copy-start(f32[12,128]{1,0:T(8,128)S(1)} %fusion) | copy-start | bytes 18436
  69.3 18.5 %copy-start.2 = (bf16[128,1536]{0,1:T(8,128)(2,1)}, bf16[128,1536]{0,1:T(8,128)(2,1)S(1)}, u32[]{:S(2)}) copy-start(bf16[128,1536]{0,1:T(8,128)(2,1)S(1)} %copy.52) | copy-start | bytes 1179652
  71.7 0.7 copy-start.5
  87.1 0.7 copy-start.9
  87.2 155.3 %reduce-scatter.5.cloned.1.call-start = ((), (), s32[]{:S(2)}) async-start(), calls=%async_computation.3 | async-start | bytes 4718592 | tf_op jit(solution)/shard_map/reduce_scatter | solution.py:103
  89.5 3.1 %copy-start.11 = (f32[128,12]{0,1:T(8,128)S(1)}, f32[128,12]{0,1:T(8,128)}, u32[]{:S(2)}) copy-start(f32[128,12]{0,1:T(8,128)} %get-tuple-element.57) | copy-start | bytes 18436
  92.5 2.1 copy-start.4
  96.2 3.4 %copy-start.1 = (f32[256,1536]{1,0:T(8,128)S(1)}, f32[256,1536]{1,0:T(8,128)}, u32[]{:S(2)}) copy-start(f32[256,1536]{1,0:T(8,128)} %copy.56) | copy-start | bytes 4718596
  103.0 1.0 copy-start.6
  103.0 176.0 %all-reduce.2.cloned.1.call-start = ((), (), s32[]{:S(2)}) async-start(), calls=%async_computation.4 | async-start | bytes 1572864 | tf_op jit(solution)/shard_map/psum | solution.py:123
Sparse Core Ops, SparseCore 0:
  10.3 55.6 all-gather.1
  87.3 109.7 reduce-scatter.6
  199.3 43.0 reduce-scatter.4
  244.6 34.3 all-reduce.1
where the time goes:
time: 289 us; the launch traced here: 288 us
  waiting for transfers between devices  180 us (62%)
  local copies, waits for them, and re-layouts  30.1 us (10%)
  blocking collectives  23.7 us (8%)
  matrix products  21.9 us (8%)
  other arithmetic  17.8 us (6%)
  between operations  14 us (5%)
    unnamed x5, waiting for transfers between devices  88.5 us
    reduce_scatter x1, waiting for transfers between devices, per_device(): lax.psum_scatter(jnp.concatenate([key_part.reshape(row_count * lax.axis_s...  41.8 us
    psum x1, waiting for transfers between devices, per_device(): weight_grad = lax.psum(grad_piece, 'seq')  34.1 us
    unnamed x30, local copies, waits for them, and re-layouts  19.9 us
    all_gather x1, waiting for transfers between devices, per_device(): full_weight = lax.all_gather(out_weight, 'dp', axis=0, tiled=True)  15.7 us
    all_gather x1, blocking collectives, per_device(): lax.all_gather(values, 'seq', axis=0, tiled=True)  12.8 us
    all_gather x1, blocking collectives, per_device(): lax.all_gather(keys, 'seq', axis=0, tiled=True)  11 us
  transfers between devices with their start and end apart: 4, of which 4 were waited for; matrix products, arithmetic and copies ran while one was open for 16% of the time, Pallas kernels for 0%

commit v1 on v0

--- a/solution.py
+++ b/solution.py
@@ -120,7 +120,8 @@
         scatter_dimension=0,
         tiled=True,
     )
-    weight_grad = lax.psum(grad_piece, "seq")
+    parts = lax.all_gather(grad_piece, "seq", axis=0, tiled=False)
+    weight_grad = parts.sum(axis=0)
     return (mixed_out, query_grad, key_grad, value_grad, weight_grad)
 
 

time: 289 us -> 276 us (0.955)
  waiting for transfers between devices: 180 us -> 171 us
  local copies, waits for them, and re-layouts: 30.1 us -> 24.7 us
    reduce_scatter x0 -> x1, waiting for transfers between devices: none -> 94 us  [per_device(): lax.psum_scatter(jnp.einsum('io,id->od', upstream, attended, preferred_el...]
    unnamed x5 -> x4, waiting for transfers between devices: 88.5 us -> 0.73 us
    psum x1 -> x0, waiting for transfers between devices: 34.1 us -> none  [per_device(): weight_grad = lax.psum(grad_piece, 'seq')]
    all_gather x0 -> x1, waiting for transfers between devices: none -> 21.8 us  [per_device(): parts = lax.all_gather(grad_piece, 'seq', axis=0, tiled=False)]
    unnamed x30 -> x28, local copies, waits for them, and re-layouts: 19.9 us -> 14.6 us
  transfers between devices with their start and end apart: 4 -> 4, of which waited for: 4 -> 4; matrix products, arithmetic and copies ran while one was open for 16% -> 15% of each run, Pallas kernels for 0% -> 0%
where the time goes in v1:
time: 276 us; the launch traced here: 275 us
  waiting for transfers between devices  171 us (62%)
  local copies, waits for them, and re-layouts  24.7 us (9%)
  blocking collectives  23.7 us (9%)
  matrix products  21.4 us (8%)
  other arithmetic  20.1 us (7%)
  between operations  14 us (5%)
    reduce_scatter x1, waiting for transfers between devices, per_device(): lax.psum_scatter(jnp.einsum('io,id->od', upstream, attended, preferred_el...  94 us
    reduce_scatter x1, waiting for transfers between devices, per_device(): lax.psum_scatter(jnp.concatenate([key_part.reshape(row_count * lax.axis_s...  39.2 us
    all_gather x1, waiting for transfers between devices, per_device(): parts = lax.all_gather(grad_piece, 'seq', axis=0, tiled=False)  21.8 us
    all_gather x1, waiting for transfers between devices, per_device(): full_weight = lax.all_gather(out_weight, 'dp', axis=0, tiled=True)  15.7 us
    unnamed x28, local copies, waits for them, and re-layouts  14.6 us
    all_gather x1, blocking collectives, per_device(): lax.all_gather(values, 'seq', axis=0, tiled=True)  12.8 us
    all_gather x1, blocking collectives, per_device(): lax.all_gather(keys, 'seq', axis=0, tiled=True)  11 us
  transfers between devices with their start and end apart: 4, of which 4 were waited for; matrix products, arithmetic and copies ran while one was open for 15% of the time, Pallas kernels for 0%

profile of v1, /device:TPU:0, one launch (start us, length us, event | category | flops | bytes accessed | tf_op | source)
XLA Modules:
  0.0 275.4 jit_solution(1486163967227236075)
XLA Ops:
  7.2 0.7 all-gather.4.cloned.1.call-update
  8.0 1.0 slice_reduce_fusion.1
  9.0 0.1 reduce
  9.1 1.2 copy.46
  10.4 1.4 copy.47
  11.8 12.8 %all_gather.16 = bf16[256,1536]{1,0:T(8,128)(2,1)S(1)} all-gather(bf16[128,1536]{1,0:T(8,128)(2,1)S(1)} %copy-done.7), channel_id=1, replica_groups=mesh['dp'=16,'seq'=2] {'seq'}, dimensions={0}, use_global_device_ids=true | all-gather | bytes 1179648 | tf_op jit(solution)/shard_map/all_gather | solution.py:56
  24.5 1.2 copy.50
  25.7 0.1 constant_dynamic-slice_fusion
  25.8 0.7 fusion.18
  26.5 2.5 fusion.16
  29.0 0.6 fusion.19
  29.6 4.4 %compare_select_fusion.1 = s32[256,1]{0,1:T(1,128)S(1)} fusion(s32[]{:T(128)} %bitcast.7, s32[]{:T(128)} %bitcast.8, s32[]{:T(128)} %bitcast.9, s32[]{:T(128)} %bitcast.10, s32[]{:T(128)} %bitcast.11, s32[]{:T(128)} %bitcast.13, s32[]{:T(128)} %bitcast.12), kind=kLoop, calls=%fused_computation.30 | loop fusion | flops 5888 | bytes 1052 | tf_op jit(solution)/shard_map/gather | solution.py:49
  34.1 0.1 fusion.15
  34.2 0.6 broadcast_select_fusion
  34.8 0.1 fusion.14
  34.9 0.1 select_reduce_fusion.3
  35.0 0.1 select_reduce_fusion
  35.1 11.0 %all_gather.15 = bf16[256,1536]{0,1:T(8,128)(2,1)S(1)} all-gather(bf16[128,1536]{0,1:T(8,128)(2,1)S(1)} %copy.47), channel_id=1, replica_groups=mesh['dp'=16,'seq'=2] {'seq'}, dimensions={0}, use_global_device_ids=true | all-gather | bytes 1179648 | tf_op jit(solution)/shard_map/all_gather | solution.py:55
  46.1 2.8 %and_select_fusion.8 = (s32[128]{0:T(128)S(1)}, s32[128]{0:T(128)S(1)}, s32[128]{0:T(128)S(1)}) fusion(s32[128]{0:T(128)S(1)} %get-tuple-element.32, s32[128]{0:T(128)S(1)} %get-tuple-element.31, s32[128]{0:T(128)S(1)} %get-tuple-element.33, s32[]{:T(128)} %bitcast.3, s32[]{:T(128)} %bitcast.2, s32[]{:T(128)} %bitcast.1, s32[]{:T(128)} %bitcast), kind=kLoop, calls=%fused_computation.61 | loop fusion | flops 7168 | bytes 3088 | tf_op jit(solution)/shard_map/jit(floor_divide)/jit(_where)/select_n | solution.py:24
  48.8 0.3 and_select_fusion.7
  49.1 0.2 fusion.13
  49.3 0.5 fusion.20
  49.8 0.5 fusion
  50.3 15.7 %all-gather.4.cloned.1.call-done = bf16[1536,1536]{1,0:T(8,128)(2,1)} async-done(((bf16[96,1536]{1,0:T(8,128)(2,1)}), bf16[1536,1536]{1,0:T(8,128)(2,1)}) %all-gather.4.cloned.1.call-update) | async-done | bytes 4718608 | tf_op jit(solution)/shard_map/all_gather | solution.py:53
  66.0 3.1 %convolution_convert_fusion = bf16[128,1536]{1,0:T(8,128)(2,1)S(1)} fusion(bf16[128,1536]{1,0:T(8,128)(2,1)S(1)} %copy-done, bf16[1536,1536]{1,0:T(8,128)(2,1)} %all-gather.4.cloned.1.call-done), kind=kOutput, calls=%fused_computation.2 | convolution fusion | flops 604176384 | bytes 5505024 | tf_op jit(solution)/shard_map/dot_general | solution.py:78
  69.1 0.2 copy.51
  69.3 2.4 multiply_reduce_fusion
  71.7 0.7 copy-done.5
  72.5 5.0 %convolution_bitcast_fusion = f32[1536,1536]{0,1:T(8,128)} fusion(bf16[128,1536]{0,1:T(8,128)(2,1)S(1)} %bitcast.71, bf16[128,1536]{1,0:T(8,128)(2,1)S(1)} %copy-done), kind=kOutput, calls=%fused_computation | convolution fusion | flops 603979776 | bytes 10223616 | tf_op jit(solution)/shard_map/io,id->od/dot_general | solution.py:118
  77.5 9.6 %copy.62 = f32[1536,1536]{1,0:T(8,128)} copy(f32[1536,1536]{0,1:T(8,128)} %convolution_bitcast_fusion) | data formatting | bytes 18874368
  87.2 0.0 reduce-scatter.5.cloned.1.call-start
  87.2 0.6 copy-done.9
  87.9 1.6 fusion.6
  89.5 3.1 %copy.55 = f32[256,1536]{1,0:T(8,128)} copy(f32[256,1536]{0,1:T(8,128)} %bitcast.62) | data formatting | bytes 3145728 | tf_op jit(solution)/shard_map/reshape | solution.py:107
  92.5 2.1 multiply_convert_fusion
  94.7 1.5 convolution_multiply_fusion
  96.2 3.4 %copy.54 = f32[256,1536]{1,0:T(8,128)} copy(f32[256,1536]{0,1:T(8,128)} %bitcast.63) | data formatting | bytes 3145728 | tf_op jit(solution)/shard_map/reshape | solution.py:106
  99.5 3.5 %pad_maximum_fusion = f32[256,3072]{1,0:T(8,128)} fusion(f32[256,1536]{1,0:T(8,128)S(1)} %copy-done.1, f32[256,1536]{1,0:T(8,128)} %copy.54), kind=kLoop, calls=%fused_computation.1 | loop fusion | flops 786432 | bytes 6291456 | tf_op jit(solution)/shard_map/concatenate | solution.py:104
  103.0 0.0 all-gather.6.cloned.1.call-start
  103.1 94.0 %reduce-scatter.7.cloned.1.call-done = f32[96,1536]{1,0:T(8,128)} async-done(((f32[1536,1536]{1,0:T(8,128)}), f32[96,1536]{1,0:T(8,128)}) %reduce-scatter.7.cloned.1.call-update) | async-done | bytes 589840 | tf_op jit(solution)/shard_map/reduce_scatter | solution.py:117
  197.1 0.4 fusion.4
  197.5 0.9 copy.57
  198.4 4.7 %convolution_convert_fusion.1 = bf16[128,1536]{1,0:T(8,128)(2,1)} fusion(bf16[128,1536]{0,1:T(8,128)(2,1)S(1)} %bitcast.72, bf16[1536,1536]{1,0:T(8,128)(2,1)} %all-gather.4.cloned.1.call-done), kind=kOutput, calls=%fused_computation.3 | convolution fusion | flops 604176384 | bytes 5505024 | tf_op jit(solution)/shard_map/id,od->io/dot_general | solution.py:75
  203.2 39.2 %reduce-scatter.5.cloned.1.call-done = f32[128,3072]{1,0:T(8,128)} async-done(((f32[256,3072]{1,0:T(8,128)}), f32[128,3072]{1,0:T(8,128)}) %reduce-scatter.5.cloned.1.call-update) | async-done | bytes 1572880 | tf_op jit(solution)/shard_map/reduce_scatter | solution.py:103
  242.4 1.5 convert.4
  243.9 0.9 fusion.17
  244.9 21.8 %all-gather.6.cloned.1.call-done = f32[192,1536]{1,0:T(8,128)} async-done(((f32[96,1536]{1,0:T(8,128)}), f32[192,1536]{1,0:T(8,128)}) %all-gather.6.cloned.1.call-update) | async-done | bytes 1179664 | tf_op jit(solution)/shard_map/all_gather | solution.py:123
  266.6 2.2 reduce_sum.109
  (33 shorter events, 0.3 us)
Async XLA Ops:
  7.2 58.8 %copy-start = (bf16[128,1536]{1,0:T(8,128)(2,1)S(1)}, bf16[128,1536]{1,0:T(8,128)(2,1)}, u32[]{:S(2)}) copy-start(bf16[128,1536]{1,0:T(8,128)(2,1)} %param.10) | copy-start | bytes 1179652
  7.2 4.6 %copy-start.7 = (bf16[128,1536]{1,0:T(8,128)(2,1)S(1)}, bf16[128,1536]{1,0:T(8,128)(2,1)}, u32[]{:S(2)}) copy-start(bf16[128,1536]{1,0:T(8,128)(2,1)} %param.9) | copy-start | bytes 1179652
  7.2 58.8 %all-gather.4.cloned.1.call-start = ((), (), s32[]{:S(2)}) async-start(), calls=%async_computation.2 | async-start | bytes 5013504 | tf_op jit(solution)/shard_map/all_gather | solution.py:53
  7.9 189.2 %reduce-scatter.7.cloned.1.call-start = ((), (), s32[]{:S(2)}) async-start(), calls=%async_computation.5 | async-start | bytes 10027008 | tf_op jit(solution)/shard_map/reduce_scatter | solution.py:117
  10.4 38.9 %copy-start.3 = (bf16[128,1536]{0,1:T(8,128)(2,1)}, bf16[128,1536]{0,1:T(8,128)(2,1)S(1)}, u32[]{:S(2)}) copy-start(bf16[128,1536]{0,1:T(8,128)(2,1)S(1)} %copy.46) | copy-start | bytes 1179652
  11.8 14.0 %copy-start.10 = (s32[1,8]{1,0:T(1,128)S(1)}, s32[1,8]{1,0:T(1,128)}, u32[]{:S(2)}) copy-start(s32[1,8]{1,0:T(1,128)} %param.13) | copy-start | bytes 100
  50.3 19.0 %copy-start.8 = (f32[12,128]{1,0:T(8,128)}, f32[12,128]{1,0:T(8,128)S(1)}, u32[]{:S(2)}) copy-start(f32[12,128]{1,0:T(8,128)S(1)} %fusion) | copy-start | bytes 18436
  69.3 18.5 %copy-start.2 = (bf16[128,1536]{0,1:T(8,128)(2,1)}, bf16[128,1536]{0,1:T(8,128)(2,1)S(1)}, u32[]{:S(2)}) copy-start(bf16[128,1536]{0,1:T(8,128)(2,1)S(1)} %copy.51) | copy-start | bytes 1179652
  71.7 0.7 copy-start.5
  87.1 0.7 copy-start.9
  87.2 155.3 %reduce-scatter.5.cloned.1.call-start = ((), (), s32[]{:S(2)}) async-start(), calls=%async_computation.3 | async-start | bytes 4718592 | tf_op jit(solution)/shard_map/reduce_scatter | solution.py:103
  89.5 3.1 %copy-start.11 = (f32[128,12]{0,1:T(8,128)S(1)}, f32[128,12]{0,1:T(8,128)}, u32[]{:S(2)}) copy-start(f32[128,12]{0,1:T(8,128)} %get-tuple-element.57) | copy-start | bytes 18436
  92.5 2.1 copy-start.4
  96.2 3.4 %copy-start.1 = (f32[256,1536]{1,0:T(8,128)S(1)}, f32[256,1536]{1,0:T(8,128)}, u32[]{:S(2)}) copy-start(f32[256,1536]{1,0:T(8,128)} %copy.55) | copy-start | bytes 4718596
  103.0 163.6 %all-gather.6.cloned.1.call-start = ((), (), s32[]{:S(2)}) async-start(), calls=%async_computation.4 | async-start | bytes 1769472 | tf_op jit(solution)/shard_map/all_gather | solution.py:123
  197.1 1.3 copy-start.6
Sparse Core Ops, SparseCore 0:
  10.3 55.6 all-gather.3
  87.3 109.7 reduce-scatter.6
  199.3 43.0 reduce-scatter.4
  243.8 22.7 all-gather.5
